TPU v7x, 256 devices: a whole 4x4x8 slice. The times are simulated.
256 devices in a mesh: dp: 2 (over z_hi), tensor: 4 (over y), pool: 32 (over x, z_lo, core).
Axes of the slice: x: 4, y: 4, z: 8 (z_hi: 2, z_lo: 4; z = z_hi * 4 + z_lo), core: 2. Of those that a mesh axis runs over, the one named last changes fastest.
Arguments:
- tokens: bfloat16 [64, 1024, 4096], P(('dp', 'pool')), may hold values from -192 to 192, as said below
- w_hidden: bfloat16 [4096, 4096], P('pool', 'tensor'), may hold values from -0.09375 to 0.09375
- w_out: bfloat16 [4096, 256], P('tensor'), may hold values from -0.09375 to 0.09375
- bank: bfloat16 [32768, 256], P('pool'), may hold values from -0.5 to 0.5
- item_ids: int32 [32768], P('pool'), may hold values from 0 to 1048575
- log_freq: bfloat16 [1048576], replicated, may hold values from -14 to -6
- positives: int32 [64, 1024], P(('dp', 'pool'), 'tensor'), may hold values from 0 to 32767
- new_items: bfloat16 [8192, 256], P('pool'), may hold values from -0.5 to 0.5
- new_owner: int32 [8192, 1], P('pool'), may hold values from 0 to 31; in each aligned block of 256 rows (0 to 255, 256 to 511, ...) at most 16 rows name the same one
- queue_head: int32 [32], P('pool'), may hold values from 0 to 1023
Outputs:
- query_loss: float32 [64, 1024], P(('dp', 'pool'), 'tensor')
- new_bank: bfloat16 [32768, 256], P('pool')
Inputs may be any that keep to these rules, and one draw needn't show every extreme that they name: `tokens`: float values within the range. `new_owner`: among the 256 new rows of one pool index, no shard is named by more than 16 rows, a bound that some block reaches.
All inputs are finite; a program needn't handle non-finite values.
Results may differ from a plain program's by a relative error of at most 0.002.
Values may be sent and summed in bfloat16 or wider, within the bound.
A program may use at most 128 MiB of HBM per device.

v0:
```python
import jax
import jax.numpy as jnp
from jax import lax
from jax.sharding import Mesh
from jax.sharding import PartitionSpec as P

POOL = ("pool_0", "pool_1", "pool_2")
DP_POOL = ("dp", "pool_0", "pool_1", "pool_2")
inv_temp = 5.0


def split_up(x, dim, count):
    before, after = (x.shape[:dim], x.shape[dim + 1 :])
    return jnp.moveaxis(x.reshape(*before, count, -1, *after), dim, 0)


def sum_at_owner(x, axis, dim):
    count = lax.axis_size(axis)
    blocks = lax.all_to_all(split_up(x, dim, count), axis, 0, 0, tiled=True)
    return jnp.sum(blocks, axis=0)


def all_in_one(x, axis):
    leaves = jax.tree.leaves(x)
    turns = sorted(range(len(leaves)), key=lambda k: -leaves[k].size)
    width = (1, *leaves[turns[0]].shape)[-1]
    lines = [
        jnp.pad(leaves[k].reshape(-1), (0, -leaves[k].size % width)).reshape(-1, width)
        for k in turns
    ]
    both, at, found = (lax.all_gather(jnp.concatenate(lines), axis), 0, {})
    for k, line in zip(turns, lines):
        section = both[:, at : at + len(line)].reshape(len(both), -1)
        found[k] = section[:, : leaves[k].size].reshape(-1, *leaves[k].shape)
        at += len(line)
    numbers = iter(range(len(leaves)))
    return jax.tree.map(lambda _: found[next(numbers)], x)


def joined_all(x, axes, combine):
    for axis in axes:
        pieces = all_in_one(x, axis)
        x = jax.tree.map(lambda part: part[0], pieces)
        for k in range(1, lax.axis_size(axis)):
            x = combine(x, jax.tree.map(lambda part: part[k], pieces))
    return x


def copy_for_each(x, axis):
    copies = jnp.broadcast_to(x, (lax.axis_size(axis), *x.shape))
    return lax.all_to_all(copies, axis, split_axis=0, concat_axis=0, tiled=True)


def folded_in_pairs(pieces, combine):
    while len(jax.tree.leaves(pieces)[0]) > 1:
        pieces = jax.vmap(combine)(*(pieces[side::2] for side in (0, 1)))
    return pieces[0]


def entering(x, axis, combine, identity):
    count, position = (lax.axis_size(axis), lax.axis_index(axis))
    passed = jnp.arange(count) < position

    def kept(part, zero, own):
        part = jnp.where(
            passed.reshape(-1, *(1 for _ in own.shape)), part, jnp.asarray(zero, own.dtype)
        )
        return part

    pieces = copy_for_each(x, axis)
    return folded_in_pairs(kept(pieces, identity, x), combine)


def local_stats(query_rows, target_rows, bank, offsets, base_column):
    row_count = query_rows.shape[0]
    bank_rows = bank.shape[0]
    block_width = 512
    block_count = bank_rows // block_width
    blocks = bank.reshape(block_count, block_width, bank.shape[1])
    shifts = offsets.reshape(block_count, block_width)

    def block_step(running, inputs):
        run_max, run_sum, run_pos = running
        bank_block, block_offsets, block_index = inputs
        logits = (
            inv_temp * jnp.dot(query_rows, bank_block.T, preferred_element_type=jnp.float32)
            - block_offsets[None, :]
        )
        next_max = jnp.maximum(run_max, jnp.max(logits, axis=1))
        run_sum = run_sum * jnp.exp(run_max - next_max) + jnp.sum(
            jnp.exp(logits - next_max[:, None]), axis=1
        )
        columns = base_column + block_index * block_width + jnp.arange(block_width, dtype=jnp.int32)
        run_pos = run_pos + jnp.sum(
            jnp.where(columns[None, :] == target_rows[:, None], logits, 0.0), axis=1
        )
        return ((next_max, run_sum, run_pos), None)

    initial = (
        jnp.full((row_count,), -jnp.inf, jnp.float32),
        jnp.zeros((row_count,), jnp.float32),
        jnp.zeros((row_count,), jnp.float32),
    )
    final, _ = lax.scan(
        block_step, initial, (blocks, shifts, jnp.arange(block_count, dtype=jnp.int32))
    )
    return final


def combine(earlier_part, later_part):
    both_max = jnp.maximum(earlier_part[0], later_part[0])
    both_sum = earlier_part[1] * jnp.exp(earlier_part[0] - both_max) + later_part[1] * jnp.exp(
        later_part[0] - both_max
    )
    return (both_max, both_sum, earlier_part[2] + later_part[2])


def add_counts(earlier_part, later_part):
    return earlier_part + later_part


def body(
    tokens, w_hidden, w_out, bank, item_ids, log_freq, positives, new_items, new_owner, queue_head
):
    token_rows = tokens[0]
    pre_act = jnp.dot(
        token_rows,
        lax.all_gather(w_hidden, POOL, axis=0, tiled=True),
        preferred_element_type=jnp.float32,
    )
    hidden = jnp.maximum(pre_act, 0.0).astype(jnp.bfloat16)
    partial_value = jnp.dot(hidden, w_out, preferred_element_type=jnp.float32)
    queries = sum_at_owner(partial_value, "tensor", 0).astype(jnp.bfloat16)
    offsets = jnp.take(log_freq, item_ids).astype(jnp.float32)
    own_index = lax.axis_index(POOL)
    base_column = own_index * bank.shape[0]
    query_piece = lax.all_gather(queries[None], POOL, axis=0, tiled=True)
    target_piece = lax.all_gather(positives, POOL, axis=0, tiled=True)
    groups_in = query_piece.shape[0]
    run_max, run_sum, run_pos = local_stats(
        query_piece.reshape(-1, query_piece.shape[2]),
        target_piece.reshape(-1),
        bank,
        offsets,
        base_column,
    )
    maxima = run_max.reshape(groups_in, -1)
    totals = run_sum.reshape(groups_in, -1)
    scores = run_pos.reshape(groups_in, -1)
    maxima, totals, scores = (maxima, totals, scores)
    maxima, totals, scores = joined_all((maxima, totals, scores), POOL, combine)
    own_max = lax.dynamic_slice_in_dim(maxima, own_index, 1, 0)
    own_sum = lax.dynamic_slice_in_dim(totals, own_index, 1, 0)
    own_pos = lax.dynamic_slice_in_dim(scores, own_index, 1, 0)
    query_loss = own_max + jnp.log(own_sum) - own_pos
    owners = new_owner[:, 0]
    head_slot = queue_head[0]
    shard_rows = bank.shape[0]
    peer_count = lax.axis_size(POOL)
    local_rows = new_items.shape[0]
    capacity = 2 * local_rows // peer_count
    onehot = (owners[:, None] == jnp.arange(peer_count, dtype=jnp.int32)[None, :]).astype(jnp.int32)
    counts = jnp.sum(onehot, axis=0, dtype=jnp.int32)
    before = jnp.sum(
        (jnp.cumsum(onehot, axis=0, dtype=jnp.int32) - onehot) * onehot, axis=1, dtype=jnp.int32
    )
    earlier = entering(counts, POOL, add_counts, jnp.zeros_like(counts))
    ranks = before + jnp.sum(onehot * earlier[None, :], axis=1, dtype=jnp.int32)
    send_pos = owners * capacity + before
    rows_out = (
        jnp.zeros((peer_count * capacity, new_items.shape[1]), jnp.bfloat16)
        .at[send_pos]
        .set(new_items)
    )
    ranks_out = jnp.full((peer_count * capacity,), -1, jnp.int32).at[send_pos].set(ranks)
    rows_in, ranks_in = (
        lax.all_to_all(
            rows_out.reshape(peer_count, capacity, -1),
            POOL,
            split_axis=0,
            concat_axis=0,
            tiled=True,
        ),
        lax.all_to_all(
            ranks_out.reshape(peer_count, capacity), POOL, split_axis=0, concat_axis=0, tiled=True
        ),
    )
    local_slots = jnp.where(ranks_in >= 0, (head_slot + ranks_in) % shard_rows, shard_rows).reshape(
        -1
    )
    new_bank = bank.at[local_slots].set(rows_in.reshape(-1, new_items.shape[1]), mode="drop")
    return (query_loss, new_bank)


def solution(mesh):
    finer = Mesh(
        mesh.devices.reshape(mesh.shape["dp"], mesh.shape["tensor"], 4, 4, 2),
        ("dp", "tensor", "pool_0", "pool_1", "pool_2"),
    )
    in_specs = (
        P(DP_POOL, None, None),
        P(POOL, "tensor"),
        P("tensor", None),
        P(POOL, None),
        P(POOL),
        P(),
        P(DP_POOL, "tensor"),
        P(POOL, None),
        P(POOL, None),
        P(POOL),
    )
    out_specs = (P(DP_POOL, "tensor"), P(POOL, None))
    return jax.shard_map(body, mesh=finer, in_specs=in_specs, out_specs=out_specs, check_vma=False)
```

profile of v0, /device:TPU:1, one launch (start us, length us, event | category | flops | bytes accessed | tf_op | source)
XLA Modules:
  0.0 274.3 jit_solution(2599973721477552642)
XLA Ops:
  7.2 0.0 copy-start
  7.2 0.0 all-gather.8.cloned.1.call-start
  7.2 0.7 all-gather.8.cloned.1.call-update
  7.9 0.0 copy-start.4
  7.9 0.0 copy-start.3
  7.9 0.0 copy-start.5
  7.9 0.0 copy-start.2
  8.0 0.0 all-gather.10.cloned.1.call-start
  8.0 74.6 %all-gather.8.cloned.1.call-done = bf16[4096,1024]{1,0:T(8,128)(2,1)} async-done(((bf16[128,1024]{1,0:T(8,128)(2,1)}), bf16[4096,1024]{1,0:T(8,128)(2,1)}) %all-gather.8.cloned.1.call-update) | async-done | bytes 8388624 | tf_op jit(solution)/shard_map/all_gather | solution.py:128
  82.6 16.4 %fusion.12 = f32[1024,256]{1,0:T(8,128)} fusion(bf16[1024,256]{1,0:T(8,128)(2,1)} %param.14, bf16[4096,1024]{1,0:T(8,128)(2,1)} %all-gather.8.cloned.1.call-done, bf16[1,1024,4096]{2,1,0:T(8,128)(2,1)} %param.12), kind=kOutput, calls=%fused_computation.22 | convolution fusion | flops 9128902656 | bytes 18350080 | tf_op jit(solution)/shard_map/dot_general | solution.py:132
  98.9 19.1 %all_to_all.28 = f32[4,256,256]{2,1,0:T(8,128)} all-to-all(f32[4,256,256]{2,1,0:T(8,128)} %bitcast.252), channel_id=1, replica_groups=mesh['dp'=2,'tensor'=4,'pool_0'=4,'pool_1'=4,'pool_2'=2] {'tensor'}, dimensions={0} | all-to-all | bytes 2097152 | tf_op jit(solution)/shard_map/all_to_all | solution.py:19
  118.0 2.0 reduce_sum.56
  120.0 0.0 all-gather.10.cloned.1.call-update
  120.0 0.0 copy-done.4
  120.0 0.1 convert_reduce_fusion
  120.2 0.6 broadcast_in_dim.52
  120.8 6.5 %all-to-all-start.1 = ((s32[32,1,32]{2,1,0:T(1,128)}), s32[32,1,32]{2,1,0:T(1,128)S(1)}, u32[]{:S(2)}, u32[]{:S(2)}) async-start(s32[32,1,32]{2,1,0:T(1,128)} %broadcast_in_dim.52), calls=%async_computation.1 | async-start | bytes 32768 | tf_op jit(solution)/shard_map/all_to_all | solution.py:51
  127.3 0.0 copy-done.3
  127.3 0.0 copy-done
  127.3 6.8 %gather_fusion = bf16[1024]{0:T(1024)(128)(2,1)S(1)} fusion(bf16[1048576]{0:T(1024)(128)(2,1)S(1)} %copy-done, s32[1024]{0:T(1024)S(1)} %fusion.46), kind=kCustom, calls=%fused_computation | custom fusion | bytes 8192 | tf_op jit(solution)/shard_map/jit(_take)/gather | solution.py:134
  134.1 0.6 reduce-window.6
  134.7 0.2 slice_reduce_fusion
  135.0 0.0 all-to-all-done.1
  135.0 0.1 broadcast_select_fusion
  135.3 0.1 select_reduce_fusion
  135.4 1.4 scatter_custom_fusion
  136.8 0.7 all_to_all.21
  137.5 7.7 %all-to-all-start.2 = ((s32[32,1,16]{2,1,0:T(1,128)}), s32[32,1,16]{2,1,0:T(1,128)S(1)}, u32[]{:S(2)}, u32[]{:S(2)}) async-start(s32[32,1,16]{2,1,0:T(1,128)} %bitcast.37), calls=%async_computation.2 | async-start | bytes 32768 | tf_op jit(solution)/shard_map/all_to_all | solution.py:184
  145.2 0.0 copy-done.5
  145.2 43.7 %all-gather.4 = s32[32,1,256]{2,1,0:T(1,128)S(1)} all-gather(s32[1,1,256]{2,1,0:T(1,128)S(1)} %bitcast.259), channel_id=1, replica_groups=mesh['dp'=2,'tensor'=4,'pool_0'=4,'pool_1'=4,'pool_2'=2] {'pool_0','pool..., dimensions={0}, use_global_device_ids=true | all-gather | bytes 33792 | tf_op jit(solution)/shard_map/all_gather | solution.py:138
  189.6 2.5 scatter_custom_fusion.1
  192.1 0.0 all-to-all-done.2
  192.1 3.7 %all-to-all-start.3 = ((bf16[32,16,256]{2,1,0:T(8,128)(2,1)}), bf16[32,16,256]{2,1,0:T(8,128)(2,1)S(1)}, u32[]{:S(2)}, u32[]{:S(2)}) async-start(bf16[32,16,256]{2,1,0:T(8,128)(2,1)} %bitcast.40), calls=%async_computation.3 | async-start | bytes 524288 | tf_op jit(solution)/shard_map/all_to_all | solution.py:177
  195.8 0.1 compare_reduce_fusion
  195.8 0.1 ge.29
  196.0 0.1 add.200
  196.1 0.0 all-gather.10.cloned.1.call-done
  196.1 0.0 copy-done.2
  196.1 37.4 %while.15 = (s32[]{:T(128)}, f32[8192]{0:T(1024)S(1)}, f32[8192]{0:T(1024)S(1)}, f32[8192]{0:T(1024)S(1)}, bf16[2,512,256]{2,1,0:T(8,128)(2,1)S(1)}, /*index=5*/...) while((s32[]{:T(128)}, f32[8192]{0:T(1024)S(1)}, ...), condition=%wide.region_5.6_spmd.clone, body=%wide.region_1.5_spmd.clone.sunk | while | flops 2181087744 | bytes 38676668 | solution.py:104
  196.2 9.2 %fusion.74 = (f32[8192]{0:T(1024)S(1)}, f32[512,8192]{1,0:T(8,128)}) fusion(f32[512]{0:T(512)S(1)} %bitcast.241, bf16[8192,256]{1,0:T(8,128)(2,1)} %get-tuple-element.234, bf16[2,512,256]{2,1,0:T(8,128)(2,1)S(1)} %get-tuple-element.233, s32[]{:T(128)S(6)} %copy.27), kind=kOutput, calls=%fused_computation.130.clone.1 | convolution fusion | flops 2160058368 | bytes 21268484 | tf_op jit(solution)/shard_map/while/body/eval_jaxpr/dot_general | solution.py:86
  205.4 0.6 dynamic_slice.94
  206.7 8.1 %fusion.75 = (f32[8192]{0:T(1024)S(1)}, f32[8192]{0:T(1024)S(1)}) fusion(f32[512,8192]{1,0:T(8,128)} %get-tuple-element.198, s32[8192]{0:T(1024)S(1)} %bitcast.242, s32[512]{0:T(512)S(1)} %iota_add_fusion.2, f32[8192]{0:T(1024)S(1)} %select_maximum_fusion.2), kind=kLoop, calls=%fused_computation.8.clone.1 | loop fusion | flops 20955136 | bytes 16910336 | tf_op jit(solution)/shard_map/while/body/eval_jaxpr/reduce_sum | solution.py:94
  214.8 9.2 %fusion.74 = (f32[8192]{0:T(1024)S(1)}, f32[512,8192]{1,0:T(8,128)}) fusion(f32[512]{0:T(512)S(1)} %bitcast.241, bf16[8192,256]{1,0:T(8,128)(2,1)} %get-tuple-element.234, bf16[2,512,256]{2,1,0:T(8,128)(2,1)S(1)} %get-tuple-element.233, s32[]{:T(128)S(6)} %copy.27), kind=kOutput, calls=%fused_computation.130.clone.1 | convolution fusion | flops 2160058368 | bytes 21268484 | tf_op jit(solution)/shard_map/while/body/eval_jaxpr/dot_general | solution.py:86
  224.1 0.6 dynamic_slice.94
  225.3 8.1 %fusion.75 = (f32[8192]{0:T(1024)S(1)}, f32[8192]{0:T(1024)S(1)}) fusion(f32[512,8192]{1,0:T(8,128)} %get-tuple-element.198, s32[8192]{0:T(1024)S(1)} %bitcast.242, s32[512]{0:T(512)S(1)} %iota_add_fusion.2, f32[8192]{0:T(1024)S(1)} %select_maximum_fusion.2), kind=kLoop, calls=%fused_computation.8.clone.1 | loop fusion | flops 20955136 | bytes 16910336 | tf_op jit(solution)/shard_map/while/body/eval_jaxpr/reduce_sum | solution.py:94
  233.6 10.9 %all-gather.1 = f32[384,256]{1,0:T(8,128)S(1)} all-gather(f32[96,256]{1,0:T(8,128)S(1)} %pad_maximum_fusion), channel_id=3, replica_groups=mesh['dp'=2,'tensor'=4,'pool_0'=4,'pool_1'=4,'pool_2'=2] {'pool_0'}, dimensions={0}, use_global_device_ids=true | all-gather | bytes 491520 | tf_op jit(solution)/shard_map/all_gather | solution.py:31
  244.6 11.7 %all-gather.2 = f32[384,256]{1,0:T(8,128)S(1)} all-gather(f32[96,256]{1,0:T(8,128)S(1)} %pad_maximum_fusion.1), channel_id=4, replica_groups=mesh['dp'=2,'tensor'=4,'pool_0'=4,'pool_1'=4,'pool_2'=2] {'pool_1'}, dimensions={0}, use_global_device_ids=true | all-gather | bytes 491520 | tf_op jit(solution)/shard_map/all_gather | solution.py:31
  256.3 7.7 %all-gather.3 = f32[192,256]{1,0:T(8,128)S(1)} all-gather(f32[96,256]{1,0:T(8,128)S(1)} %pad_maximum_fusion.2), channel_id=5, replica_groups=mesh['dp'=2,'tensor'=4,'pool_0'=4,'pool_1'=4,'pool_2'=2] {'pool_2'}, dimensions={0}, use_global_device_ids=true | all-gather | bytes 294912 | tf_op jit(solution)/shard_map/all_gather | solution.py:31
  264.0 0.0 all-to-all-done.3
  264.1 2.6 scatter_fusion
  266.7 0.0 copy-start.1
  266.7 0.7 fusion.54
  267.4 0.1 copy-done.1
  (53 shorter events, 0.7 us)
Async XLA Ops:
  7.2 120.1 %copy-start = (bf16[1048576]{0:T(1024)(128)(2,1)S(1)}, bf16[1048576]{0:T(1024)(128)(2,1)}, u32[]{:S(2)}) copy-start(bf16[1048576]{0:T(1024)(128)(2,1)} %param.17) | copy-start | bytes 6291460
  7.2 75.4 %all-gather.8.cloned.1.call-start = ((), (), s32[]{:S(2)}) async-start(), calls=%async_computation.4 | async-start | bytes 8650752 | tf_op jit(solution)/shard_map/all_gather | solution.py:128
  7.9 112.1 %copy-start.4 = (s32[256,1]{0,1:T(1,128)S(1)}, s32[256,1]{0,1:T(1,128)}, u32[]{:S(2)}) copy-start(s32[256,1]{0,1:T(1,128)} %param.20) | copy-start | bytes 3076
  7.9 119.3 %copy-start.3 = (s32[1024]{0:T(1024)S(1)}, s32[1024]{0:T(1024)}, u32[]{:S(2)}) copy-start(s32[1024]{0:T(1024)} %param.16) | copy-start | bytes 12292
  7.9 137.2 %copy-start.5 = (s32[1,256]{1,0:T(1,128)S(1)}, s32[1,256]{1,0:T(1,128)}, u32[]{:S(2)}) copy-start(s32[1,256]{1,0:T(1,128)} %param.18) | copy-start | bytes 3076
  7.9 188.2 %copy-start.2 = (bf16[1024,256]{1,0:T(8,128)(2,1)S(1)}, bf16[1024,256]{1,0:T(8,128)(2,1)}, u32[]{:S(2)}) copy-start(bf16[1024,256]{1,0:T(8,128)(2,1)} %param.15) | copy-start | bytes 1572868
  8.0 188.2 %all-gather.10.cloned.1.call-start = ((), (), s32[]{:S(2)}) async-start(), calls=%async_computation.5 | async-start | bytes 4325376 | tf_op jit(solution)/shard_map/all_gather | solution.py:137
  120.8 14.2 %all-to-all-start.1 = ((s32[32,1,32]{2,1,0:T(1,128)}), s32[32,1,32]{2,1,0:T(1,128)S(1)}, u32[]{:S(2)}, u32[]{:S(2)}) async-start(s32[32,1,32]{2,1,0:T(1,128)} %broadcast_in_dim.52), calls=%async_computation.1 | async-start | bytes 32768 | tf_op jit(solution)/shard_map/all_to_all | solution.py:51
  137.5 54.6 %all-to-all-start.2 = ((s32[32,1,16]{2,1,0:T(1,128)}), s32[32,1,16]{2,1,0:T(1,128)S(1)}, u32[]{:S(2)}, u32[]{:S(2)}) async-start(s32[32,1,16]{2,1,0:T(1,128)} %bitcast.37), calls=%async_computation.2 | async-start | bytes 32768 | tf_op jit(solution)/shard_map/all_to_all | solution.py:184
  192.1 72.0 %all-to-all-start.3 = ((bf16[32,16,256]{2,1,0:T(8,128)(2,1)}), bf16[32,16,256]{2,1,0:T(8,128)(2,1)S(1)}, u32[]{:S(2)}, u32[]{:S(2)}) async-start(bf16[32,16,256]{2,1,0:T(8,128)(2,1)} %bitcast.40), calls=%async_computation.3 | async-start | bytes 524288 | tf_op jit(solution)/shard_map/all_to_all | solution.py:177
  266.7 0.8 copy-start.1
Sparse Core Ops, SparseCore 0:
  9.8 72.6 all-gather.7
  120.2 60.7 all-gather.9
where the time goes:
time: 275 us; the launch traced here: 274 us
  blocking collectives  93.1 us (34%)
  waiting for transfers between devices  75.3 us (27%)
  matrix products  34.8 us (13%)
  other arithmetic  20.1 us (7%)
  starting transfers between devices  17.9 us (7%)
  local copies, waits for them, and re-layouts  16.6 us (6%)
  between operations  15 us (5%)
    all_gather x1, waiting for transfers between devices, body(): lax.all_gather(w_hidden, POOL, axis=0, tiled=True)  74.6 us
    all_gather x1, blocking collectives, body(): target_piece = lax.all_gather(positives, POOL, axis=0, tiled=True)  43.7 us
    all_gather x3, blocking collectives, all_in_one(): both, at, found = (lax.all_gather(jnp.concatenate(lines), axis), 0, {})  30.3 us
    all_to_all x1, blocking collectives, sum_at_owner(): blocks = lax.all_to_all(split_up(x, dim, count), axis, 0, 0, tiled=True)  19.1 us
    dot_general x2, matrix products, block_step(): jnp.dot(query_rows, bank_block.T, preferred_element_type=jnp.float32)  18.5 us
    dot_general x1, matrix products, body(): partial_value = jnp.dot(hidden, w_out, preferred_element_type=jnp.float32)  16.4 us
    reduce_sum x2, other arithmetic, block_step(): jnp.sum(jnp.where(columns[None, :] == target_rows[:, None], logits, 0.0),...  16.2 us
    all_to_all x1, starting transfers between devices, body(): lax.all_to_all(ranks_out.reshape(peer_count, capacity), POOL, split_axis=...  7.69 us
  transfers between devices with their start and end apart: 5, of which 1 were waited for; matrix products, arithmetic and copies ran while one was open for 18% of the time, Pallas kernels for 0%

commit v1 on v0

--- a/solution.py
+++ b/solution.py
@@ -135,7 +135,8 @@
     own_index = lax.axis_index(POOL)
     base_column = own_index * bank.shape[0]
     query_piece = lax.all_gather(queries[None], POOL, axis=0, tiled=True)
-    target_piece = lax.all_gather(positives, POOL, axis=0, tiled=True)
+    stack = jnp.stack([positives] * lax.axis_size(POOL))
+    target_piece = jnp.concatenate(lax.all_to_all(stack, POOL, 0, 0), axis=0)
     groups_in = query_piece.shape[0]
     run_max, run_sum, run_pos = local_stats(
         query_piece.reshape(-1, query_piece.shape[2]),

time: 275 us -> 261 us (0.949)
  blocking collectives: 93.1 us -> 48.1 us
  waiting for transfers between devices: 75.3 us -> 101 us
  starting transfers between devices: 17.9 us -> 22.6 us
    all_gather x1 -> x0, blocking collectives: 43.7 us -> none  [body(): target_piece = lax.all_gather(positives, POOL, axis=0, tiled=True)]
    all_gather x1, waiting for transfers between devices: 0.02 us -> 14.4 us  [body(): query_piece = lax.all_gather(queries[None], POOL, axis=0, tiled=True)]
    all_to_all x0 -> x1, waiting for transfers between devices: none -> 7.47 us  [body(): target_piece = jnp.concatenate(lax.all_to_all(stack, POOL, 0, 0), axis=0)]
    all_to_all x0 -> x1, starting transfers between devices: none -> 4.42 us  [body(): target_piece = jnp.concatenate(lax.all_to_all(stack, POOL, 0, 0), axis=0)]
    all_to_all x1, waiting for transfers between devices: 0.01 us -> 4.03 us  [body(): lax.all_to_all(ranks_out.reshape(peer_count, capacity), POOL, split_axis=...]
  transfers between devices with their start and end apart: 5 -> 6, of which waited for: 1 -> 4; matrix products, arithmetic and copies ran while one was open for 18% -> 19% of each run, Pallas kernels for 0% -> 0%
where the time goes in v1:
time: 261 us; the launch traced here: 260 us
  waiting for transfers between devices  101 us (39%)
  blocking collectives  48.1 us (18%)
  matrix products  34.8 us (13%)
  starting transfers between devices  22.6 us (9%)
  other arithmetic  20.1 us (8%)
  local copies, waits for them, and re-layouts  17.2 us (7%)
  between operations  15 us (6%)
    all_gather x1, waiting for transfers between devices, body(): lax.all_gather(w_hidden, POOL, axis=0, tiled=True)  74.6 us
    all_gather x3, blocking collectives, all_in_one(): both, at, found = (lax.all_gather(jnp.concatenate(lines), axis), 0, {})  29.1 us
    all_to_all x1, blocking collectives, sum_at_owner(): blocks = lax.all_to_all(split_up(x, dim, count), axis, 0, 0, tiled=True)  19.1 us
    dot_general x2, matrix products, block_step(): jnp.dot(query_rows, bank_block.T, preferred_element_type=jnp.float32)  18.5 us
    dot_general x1, matrix products, body(): partial_value = jnp.dot(hidden, w_out, preferred_element_type=jnp.float32)  16.4 us
    reduce_sum x2, other arithmetic, block_step(): jnp.sum(jnp.where(columns[None, :] == target_rows[:, None], logits, 0.0),...  16.2 us
    all_gather x1, waiting for transfers between devices, body(): query_piece = lax.all_gather(queries[None], POOL, axis=0, tiled=True)  14.4 us
    all_to_all x1, starting transfers between devices, body(): lax.all_to_all(ranks_out.reshape(peer_count, capacity), POOL, split_axis=...  7.69 us
  transfers between devices with their start and end apart: 6, of which 4 were waited for; matrix products, arithmetic and copies ran while one was open for 19% of the time, Pallas kernels for 0%

profile of v1, /device:TPU:1, one launch (start us, length us, event | category | flops | bytes accessed | tf_op | source)
XLA Modules:
  0.0 260.4 jit_solution(15884594271014106948)
XLA Ops:
  7.2 0.0 copy-start
  7.2 0.0 all-gather.7.cloned.1.call-start
  7.2 0.7 all-gather.7.cloned.1.call-update
  7.9 0.0 copy-start.4
  7.9 0.0 copy-start.3
  7.9 0.0 copy-start.5
  7.9 0.0 copy-start.2
  8.0 0.0 all-gather.9.cloned.1.call-start
  8.0 74.6 %all-gather.7.cloned.1.call-done = bf16[4096,1024]{1,0:T(8,128)(2,1)} async-done(((bf16[128,1024]{1,0:T(8,128)(2,1)}), bf16[4096,1024]{1,0:T(8,128)(2,1)}) %all-gather.7.cloned.1.call-update) | async-done | bytes 8388624 | tf_op jit(solution)/shard_map/all_gather | solution.py:128
  82.6 16.4 %fusion.12 = f32[1024,256]{1,0:T(8,128)} fusion(bf16[1024,256]{1,0:T(8,128)(2,1)} %param.14, bf16[4096,1024]{1,0:T(8,128)(2,1)} %all-gather.7.cloned.1.call-done, bf16[1,1024,4096]{2,1,0:T(8,128)(2,1)} %param.12), kind=kOutput, calls=%fused_computation.22 | convolution fusion | flops 9128902656 | bytes 18350080 | tf_op jit(solution)/shard_map/dot_general | solution.py:132
  98.9 19.1 %all_to_all.33 = f32[4,256,256]{2,1,0:T(8,128)} all-to-all(f32[4,256,256]{2,1,0:T(8,128)} %bitcast.244), channel_id=1, replica_groups=mesh['dp'=2,'tensor'=4,'pool_0'=4,'pool_1'=4,'pool_2'=2] {'tensor'}, dimensions={0} | all-to-all | bytes 2097152 | tf_op jit(solution)/shard_map/all_to_all | solution.py:19
  118.0 2.0 reduce_sum.56
  120.0 0.0 all-gather.9.cloned.1.call-update
  120.0 0.0 copy-done.4
  120.0 0.1 convert_reduce_fusion
  120.2 0.6 broadcast_in_dim.52
  120.8 6.5 %all-to-all-start.2 = ((s32[32,1,32]{2,1,0:T(1,128)}), s32[32,1,32]{2,1,0:T(1,128)S(1)}, u32[]{:S(2)}, u32[]{:S(2)}) async-start(s32[32,1,32]{2,1,0:T(1,128)} %broadcast_in_dim.52), calls=%async_computation.2 | async-start | bytes 32768 | tf_op jit(solution)/shard_map/all_to_all | solution.py:51
  127.3 0.6 reduce-window.6
  127.9 0.2 slice_reduce_fusion
  128.1 0.0 copy-done.3
  128.1 0.0 copy-done
  128.1 6.8 %gather_fusion = bf16[1024]{0:T(1024)(128)(2,1)S(1)} fusion(bf16[1048576]{0:T(1024)(128)(2,1)S(1)} %copy-done, s32[1024]{0:T(1024)S(1)} %fusion.46), kind=kCustom, calls=%fused_computation | custom fusion | bytes 8192 | tf_op jit(solution)/shard_map/jit(_take)/gather | solution.py:134
  135.0 0.0 all-to-all-done.2
  135.0 0.1 broadcast_select_fusion
  135.2 0.1 select_reduce_fusion
  135.4 1.4 scatter_custom_fusion
  136.8 0.7 all_to_all.25
  137.4 7.7 %all-to-all-start.3 = ((s32[32,1,16]{2,1,0:T(1,128)}), s32[32,1,16]{2,1,0:T(1,128)S(1)}, u32[]{:S(2)}, u32[]{:S(2)}) async-start(s32[32,1,16]{2,1,0:T(1,128)} %bitcast.37), calls=%async_computation.3 | async-start | bytes 32768 | tf_op jit(solution)/shard_map/all_to_all | solution.py:185
  145.8 2.5 scatter_custom_fusion.1
  148.3 4.0 %all-to-all-done.3 = s32[32,1,16]{2,1,0:T(1,128)S(1)} async-done(((s32[32,1,16]{2,1,0:T(1,128)}), s32[32,1,16]{2,1,0:T(1,128)S(1)}, u32[]{:S(2)}, u32[]{:S(2)}) %all-to-all-start.3) | async-done | bytes 2080 | tf_op jit(solution)/shard_map/all_to_all | solution.py:185
  152.4 0.0 copy-done.5
  152.4 0.6 stack.2
  153.0 4.4 %all-to-all-start.1 = ((s32[32,1,256]{2,1,0:T(1,128)}), s32[32,1,256]{2,1,0:T(1,128)S(1)}, u32[]{:S(2)}, u32[]{:S(2)}) async-start(s32[32,1,256]{2,1,0:T(1,128)} %stack.2), calls=%async_computation.1 | async-start | bytes 65536 | tf_op jit(solution)/shard_map/all_to_all | solution.py:139
  157.4 0.1 compare_reduce_fusion
  157.5 0.1 ge.29
  157.6 0.1 add.200
  157.7 7.5 %all-to-all-done.1 = s32[32,1,256]{2,1,0:T(1,128)S(1)} async-done(((s32[32,1,256]{2,1,0:T(1,128)}), s32[32,1,256]{2,1,0:T(1,128)S(1)}, u32[]{:S(2)}, u32[]{:S(2)}) %all-to-all-start.1) | async-done | bytes 32800 | tf_op jit(solution)/shard_map/all_to_all | solution.py:139
  165.2 3.9 %all-to-all-start.4 = ((bf16[32,16,256]{2,1,0:T(8,128)(2,1)}), bf16[32,16,256]{2,1,0:T(8,128)(2,1)S(1)}, u32[]{:S(2)}, u32[]{:S(2)}) async-start(bf16[32,16,256]{2,1,0:T(8,128)(2,1)} %bitcast.40), calls=%async_computation.4 | async-start | bytes 524288 | tf_op jit(solution)/shard_map/all_to_all | solution.py:178
  169.1 14.4 %all-gather.9.cloned.1.call-done = bf16[8192,256]{1,0:T(8,128)(2,1)} async-done(((bf16[256,256]{1,0:T(8,128)(2,1)}), bf16[8192,256]{1,0:T(8,128)(2,1)}) %all-gather.9.cloned.1.call-update) | async-done | bytes 4194320 | tf_op jit(solution)/shard_map/all_gather | solution.py:137
  183.6 0.0 copy-done.2
  183.6 37.3 %while.15 = (s32[]{:T(128)}, f32[8192]{0:T(1024)S(1)}, f32[8192]{0:T(1024)S(1)}, f32[8192]{0:T(1024)S(1)}, bf16[2,512,256]{2,1,0:T(8,128)(2,1)S(1)}, /*index=5*/...) while((s32[]{:T(128)}, f32[8192]{0:T(1024)S(1)}, ...), condition=%wide.region_5.6_spmd.clone, body=%wide.region_1.5_spmd.clone.sunk | while | flops 2181087744 | bytes 38611132 | solution.py:104
  183.6 9.2 %fusion.74 = (f32[8192]{0:T(1024)S(1)}, f32[512,8192]{1,0:T(8,128)}) fusion(f32[512]{0:T(512)S(1)} %bitcast.235, bf16[8192,256]{1,0:T(8,128)(2,1)} %get-tuple-element.234, bf16[2,512,256]{2,1,0:T(8,128)(2,1)S(1)} %get-tuple-element.233, s32[]{:T(128)S(6)} %copy.21), kind=kOutput, calls=%fused_computation.129.clone.1 | convolution fusion | flops 2160058368 | bytes 21268484 | tf_op jit(solution)/shard_map/while/body/eval_jaxpr/dot_general | solution.py:86
  192.8 0.6 dynamic_slice.94
  194.0 8.1 %fusion.75 = (f32[8192]{0:T(1024)S(1)}, f32[8192]{0:T(1024)S(1)}) fusion(f32[512,8192]{1,0:T(8,128)} %get-tuple-element.198, s32[8192]{0:T(1024)S(1)} %bitcast.240, s32[512]{0:T(512)S(1)} %iota_add_fusion.2, f32[8192]{0:T(1024)S(1)} %select_maximum_fusion.2), kind=kLoop, calls=%fused_computation.8.clone.1 | loop fusion | flops 20955136 | bytes 16910336 | tf_op jit(solution)/shard_map/while/body/eval_jaxpr/reduce_sum | solution.py:94
  202.2 9.2 %fusion.74 = (f32[8192]{0:T(1024)S(1)}, f32[512,8192]{1,0:T(8,128)}) fusion(f32[512]{0:T(512)S(1)} %bitcast.235, bf16[8192,256]{1,0:T(8,128)(2,1)} %get-tuple-element.234, bf16[2,512,256]{2,1,0:T(8,128)(2,1)S(1)} %get-tuple-element.233, s32[]{:T(128)S(6)} %copy.21), kind=kOutput, calls=%fused_computation.129.clone.1 | convolution fusion | flops 2160058368 | bytes 21268484 | tf_op jit(solution)/shard_map/while/body/eval_jaxpr/dot_general | solution.py:86
  211.4 0.6 dynamic_slice.94
  212.7 8.1 %fusion.75 = (f32[8192]{0:T(1024)S(1)}, f32[8192]{0:T(1024)S(1)}) fusion(f32[512,8192]{1,0:T(8,128)} %get-tuple-element.198, s32[8192]{0:T(1024)S(1)} %bitcast.240, s32[512]{0:T(512)S(1)} %iota_add_fusion.2, f32[8192]{0:T(1024)S(1)} %select_maximum_fusion.2), kind=kLoop, calls=%fused_computation.8.clone.1 | loop fusion | flops 20955136 | bytes 16910336 | tf_op jit(solution)/shard_map/while/body/eval_jaxpr/reduce_sum | solution.py:94
  220.9 9.6 %all-gather.1 = f32[384,256]{1,0:T(8,128)S(1)} all-gather(f32[96,256]{1,0:T(8,128)S(1)} %pad_maximum_fusion), channel_id=3, replica_groups=mesh['dp'=2,'tensor'=4,'pool_0'=4,'pool_1'=4,'pool_2'=2] {'pool_0'}, dimensions={0}, use_global_device_ids=true | all-gather | bytes 491520 | tf_op jit(solution)/shard_map/all_gather | solution.py:31
  230.6 11.8 %all-gather.2 = f32[384,256]{1,0:T(8,128)S(1)} all-gather(f32[96,256]{1,0:T(8,128)S(1)} %pad_maximum_fusion.1), channel_id=4, replica_groups=mesh['dp'=2,'tensor'=4,'pool_0'=4,'pool_1'=4,'pool_2'=2] {'pool_1'}, dimensions={0}, use_global_device_ids=true | all-gather | bytes 491520 | tf_op jit(solution)/shard_map/all_gather | solution.py:31
  242.5 7.6 %all-gather.3 = f32[192,256]{1,0:T(8,128)S(1)} all-gather(f32[96,256]{1,0:T(8,128)S(1)} %pad_maximum_fusion.2), channel_id=5, replica_groups=mesh['dp'=2,'tensor'=4,'pool_0'=4,'pool_1'=4,'pool_2'=2] {'pool_2'}, dimensions={0}, use_global_device_ids=true | all-gather | bytes 294912 | tf_op jit(solution)/shard_map/all_gather | solution.py:31
  250.2 0.0 all-to-all-done.4
  250.2 2.6 %scatter_fusion = bf16[1024,256]{1,0:T(8,128)(2,1)S(1)} fusion(bf16[1024,256]{1,0:T(8,128)(2,1)S(1)} %bitcast.233, s32[512]{0:T(512)S(1)} %bitcast.250, bf16[512,256]{1,0:T(8,128)(2,1)S(1)} %bitcast.243), kind=kCustom, calls=%fused_computation.3 | custom fusion | bytes 788480 | tf_op jit(solution)/shard_map/scatter | solution.py:192
  252.8 0.0 copy-start.1
  252.8 0.7 fusion.54
  253.5 0.1 copy-done.1
  (50 shorter events, 0.6 us)
Async XLA Ops:
  7.2 121.0 %copy-start = (bf16[1048576]{0:T(1024)(128)(2,1)S(1)}, bf16[1048576]{0:T(1024)(128)(2,1)}, u32[]{:S(2)}) copy-start(bf16[1048576]{0:T(1024)(128)(2,1)} %param.17) | copy-start | bytes 6291460
  7.2 75.4 %all-gather.7.cloned.1.call-start = ((), (), s32[]{:S(2)}) async-start(), calls=%async_computation.5 | async-start | bytes 8650752 | tf_op jit(solution)/shard_map/all_gather | solution.py:128
  7.9 112.1 %copy-start.4 = (s32[256,1]{0,1:T(1,128)S(1)}, s32[256,1]{0,1:T(1,128)}, u32[]{:S(2)}) copy-start(s32[256,1]{0,1:T(1,128)} %param.20) | copy-start | bytes 3076
  7.9 120.1 %copy-start.3 = (s32[1024]{0:T(1024)S(1)}, s32[1024]{0:T(1024)}, u32[]{:S(2)}) copy-start(s32[1024]{0:T(1024)} %param.16) | copy-start | bytes 12292
  7.9 144.4 %copy-start.5 = (s32[1,256]{1,0:T(1,128)S(1)}, s32[1,256]{1,0:T(1,128)}, u32[]{:S(2)}) copy-start(s32[1,256]{1,0:T(1,128)} %param.18) | copy-start | bytes 3076
  7.9 175.6 %copy-start.2 = (bf16[1024,256]{1,0:T(8,128)(2,1)S(1)}, bf16[1024,256]{1,0:T(8,128)(2,1)}, u32[]{:S(2)}) copy-start(bf16[1024,256]{1,0:T(8,128)(2,1)} %param.15) | copy-start | bytes 1572868
  8.0 175.6 %all-gather.9.cloned.1.call-start = ((), (), s32[]{:S(2)}) async-start(), calls=%async_computation.6 | async-start | bytes 4325376 | tf_op jit(solution)/shard_map/all_gather | solution.py:137
  120.8 14.2 %all-to-all-start.2 = ((s32[32,1,32]{2,1,0:T(1,128)}), s32[32,1,32]{2,1,0:T(1,128)S(1)}, u32[]{:S(2)}, u32[]{:S(2)}) async-start(s32[32,1,32]{2,1,0:T(1,128)} %broadcast_in_dim.52), calls=%async_computation.2 | async-start | bytes 32768 | tf_op jit(solution)/shard_map/all_to_all | solution.py:51
  137.4 14.9 %all-to-all-start.3 = ((s32[32,1,16]{2,1,0:T(1,128)}), s32[32,1,16]{2,1,0:T(1,128)S(1)}, u32[]{:S(2)}, u32[]{:S(2)}) async-start(s32[32,1,16]{2,1,0:T(1,128)} %bitcast.37), calls=%async_computation.3 | async-start | bytes 32768 | tf_op jit(solution)/shard_map/all_to_all | solution.py:185
  153.0 12.2 %all-to-all-start.1 = ((s32[32,1,256]{2,1,0:T(1,128)}), s32[32,1,256]{2,1,0:T(1,128)S(1)}, u32[]{:S(2)}, u32[]{:S(2)}) async-start(s32[32,1,256]{2,1,0:T(1,128)} %stack.2), calls=%async_computation.1 | async-start | bytes 65536 | tf_op jit(solution)/shard_map/all_to_all | solution.py:139
  165.2 85.0 %all-to-all-start.4 = ((bf16[32,16,256]{2,1,0:T(8,128)(2,1)}), bf16[32,16,256]{2,1,0:T(8,128)(2,1)S(1)}, u32[]{:S(2)}, u32[]{:S(2)}) async-start(bf16[32,16,256]{2,1,0:T(8,128)(2,1)} %bitcast.40), calls=%async_computation.4 | async-start | bytes 524288 | tf_op jit(solution)/shard_map/all_to_all | solution.py:178
  252.8 0.8 copy-start.1
Sparse Core Ops, SparseCore 0:
  9.8 72.6 all-gather.6
  120.2 63.3 all-gather.8
